TPU v7x, 32 devices: a whole 2x2x4 slice. The times are simulated.
32 devices in a mesh: wide: 4 (over y, x), grp: 8 (over z, core).
Axes of the slice: x: 2, y: 2, z: 4, core: 2. Of those that a mesh axis runs over, the one named last changes fastest.
Arguments:
- shapes: float32 [64, 3, 312], P(('wide', 'grp')), may hold values from -10 to 10
- density: float32 [64, 3, 312], P(('wide', 'grp')), may hold values from -6 to 6
- quad_weight: float32 [64, 312], P(('wide', 'grp')), may hold values from 0.013 to 0.13
- live: int32 [64], P(('wide', 'grp')), may hold values from 0 to 1, as said below
- neighbor: int32 [64, 64], P(('wide', 'grp')), may hold values from 0 to 1
- rotation: bfloat16 [312, 312], replicated, may hold values from 0 to 1
Outputs:
- self_ops: bfloat16 [64, 3, 312, 3, 312], P(('wide', 'grp'))
- velocity: float32 [64, 3, 312], P(('wide', 'grp'))
Inputs may be any that keep to these rules, and one draw needn't show every extreme that they name: Exactly 8 of the 16 slots held by the devices of one index of wide are live.
All inputs are finite; a program needn't handle non-finite values.
Results may differ from a plain program's by a relative error of at most 0.0036.
Values may be sent and summed in bfloat16 or wider, within the bound.
A program may use at most 64 MiB of HBM per device.

v0:
```python
import functools
import jax
import jax.numpy as jnp
from jax import lax
from jax.experimental import pallas as pl
from jax.experimental.pallas import tpu as pltpu
from jax.sharding import PartitionSpec as P

soft_square = 0.0625
MESH = pl.DeviceIdType.MESH
SYM = ((0, 0), (0, 1), (0, 2), (1, 1), (1, 2), (2, 2))


def up(value, step):
    return (value + step - 1) // step * step


def split3(x):
    hi = x.astype(jnp.bfloat16)
    rest = x - hi.astype(jnp.float32)
    mid = rest.astype(jnp.bfloat16)
    low = (rest - mid.astype(jnp.float32)).astype(jnp.bfloat16)
    return hi, mid, low


def gather_kernel(
    slots, grp, wide, rows, chunk, stride, packs,
    shape_ref, dens_ref, qw_ref, live_ref, nbr_ref, rot_ref,
    ops_ref, vel_ref, tgt_ref, src_ref, list_ref,
    ops_buf, ops_sem, own, mats, parts, gbuf, cbuf, kern, cols, table, sums, gsend, grecv, csend, crecv,
):
    n = rot_ref.shape[0]
    lanes = own.shape[1]
    span = parts.shape[2]
    caps = nbr_ref.shape[1]
    me_g = lax.axis_index("grp")
    me_w = lax.axis_index("wide")
    me = me_w * grp + me_g
    barrier = pltpu.get_barrier_semaphore()
    peers = [(dw, dg) for dw in range(wide) for dg in range(grp) if dw or dg]

    def place(dw, dg):
        return {"wide": lax.rem(me_w + dw, wide), "grp": lax.rem(me_g + dg, grp)}

    for dw, dg in peers:
        pl.semaphore_signal(barrier, inc=1, device_id=place(dw, dg), device_id_type=MESH)

    own[...] = jnp.zeros_like(own)
    mats[...] = jnp.zeros_like(mats)
    alive = [live_ref[c].astype(jnp.float32) for c in range(slots)]
    for c in range(slots):
        for a in range(3):
            row = shape_ref[a, c : c + 1, :]
            own[a * slots + c : a * slots + c + 1, 0:n] = row
            mats[c, a : a + 1, 0:n] = row
            mats[c, 3 + a : 4 + a, 0:n] = qw_ref[c : c + 1, :] * dens_ref[a, c : c + 1, :] * alive[c]
        own[3 * slots + c : 3 * slots + c + 1, 0:caps] = (
            nbr_ref[c : c + 1, :].astype(jnp.float32) * alive[c]
        )
    lane = lax.broadcasted_iota(jnp.int32, (1, span), 1)
    tag = jnp.zeros((1, span), jnp.float32)
    for c in range(slots):
        tag = jnp.where(lane == packs * stride + c, alive[c], tag)
    for g in range(grp):
        for r in range(parts.shape[1]):
            made = tag
            for q in range(packs):
                c, k = divmod(r * packs + q, 6)
                if c < slots:
                    moved = pltpu.roll(mats[c], (q * stride - g * chunk) % lanes, axis=1)
                    inside = (lane >= q * stride) & (lane < q * stride + chunk)
                    made = jnp.where(inside, moved[k : k + 1, 0:span], made)
            parts[g, r : r + 1, :] = made

    pl.semaphore_wait(barrier, len(peers))
    copies = []
    for dg in range(1, grp):
        copies.append(
            pltpu.make_async_remote_copy(
                src_ref=own,
                dst_ref=gbuf.at[me_g],
                send_sem=gsend.at[dg],
                recv_sem=grecv.at[dg],
                device_id=place(0, dg),
                device_id_type=MESH,
            )
        )
    for dw, dg in peers:
        copies.append(
            pltpu.make_async_remote_copy(
                src_ref=parts.at[lax.rem(me_g + dg, grp)],
                dst_ref=cbuf.at[me],
                send_sem=csend.at[dw * grp + dg],
                recv_sem=crecv.at[dw * grp + dg],
                device_id=place(dw, dg),
                device_id_type=MESH,
            )
        )
    for copy in copies:
        copy.start()

    rot = rot_ref[...]
    table[...] = jnp.zeros_like(table)
    table[:, 0:n] = rot
    few = lax.broadcasted_iota(jnp.int32, (n, 8), 1)
    tall = lax.broadcasted_iota(jnp.int32, (kern.shape[1], 8), 1)
    for c in range(slots):
        pos = jnp.concatenate([shape_ref[a, c : c + 1, :] for a in range(3)], axis=0)
        nodes = None
        for piece in split3(pos):
            part = lax.dot_general(
                piece, rot, (((1,), (1,)), ((), ())), preferred_element_type=jnp.float32
            )
            nodes = part if nodes is None else nodes + part
        weight = qw_ref[c : c + 1, :]
        cols[...] = jnp.transpose(mats[c])
        force = [dens_ref[b, c : c + 1, :] for b in range(3)]
        force = jnp.concatenate(force + force + [jnp.zeros((2, n), jnp.float32)], axis=0)
        force = jnp.concatenate([force, jnp.zeros((8, lanes - n), jnp.float32)], axis=1)
        turned = jnp.transpose(force)[0:n].astype(jnp.bfloat16)
        pushed = jnp.dot(rot, turned, preferred_element_type=jnp.float32)
        coarse = pushed.astype(jnp.bfloat16).astype(jnp.float32)
        table[:, lanes : lanes + 8] = jnp.where(few < 3, coarse, pushed - coarse).astype(jnp.bfloat16)

        def block_step(step, carry):
            start = pl.multiple_of(step * 16, 16)
            block = cols[pl.ds(start, 16), :]
            diff = [block[:, a : a + 1] - nodes[a : a + 1, :] for a in range(3)]
            dist = diff[0] * diff[0] + diff[1] * diff[1] + diff[2] * diff[2]
            inv = lax.rsqrt(dist + soft_square)
            scaled = inv * inv * inv * weight
            half = [d * scaled for d in diff]
            diag = (dist + 2.0 * soft_square) * scaled
            for index, (a, b) in enumerate(SYM):
                value = half[a] * diff[b]
                if a == b:
                    value = value + diag
                kern[index, pl.ds(start, 16), :] = value.astype(jnp.bfloat16)
            return carry

        steps = kern.shape[1] // 16
        lax.fori_loop(0, steps, block_step, 0, unroll=4 if steps % 4 == 0 else 1)
        total = [jnp.zeros((kern.shape[1], 8), jnp.float32) for _ in range(3)]
        for index, (a, b) in enumerate(SYM):
            product = jnp.dot(kern[index], table[...], preferred_element_type=jnp.float32)
            ops_buf[c, index] = jnp.where(alive[c] > 0.0, product[:n, :n], 0.0).astype(jnp.bfloat16)
            column = product[:, lanes : lanes + 8]
            total[a] = total[a] + jnp.where((tall == b) | (tall == 3 + b), column, 0.0)
            if a != b:
                total[b] = total[b] + jnp.where((tall == a) | (tall == 3 + a), column, 0.0)
        for a in range(3):
            sums[...] = jnp.zeros_like(sums)
            sums[0 : kern.shape[1], :] = total[a]
            row = jnp.sum(jnp.transpose(sums[...]), axis=0, keepdims=True)
            vel_ref[a, c : c + 1, :] = row[:, :n]
        store = pltpu.make_async_copy(ops_buf.at[c], ops_ref.at[c], ops_sem.at[c])
        store.start()
        copies.append(store)

    gbuf[me_g] = own[...]
    cbuf[me] = parts[me_g]
    for copy in copies:
        copy.wait()
    tgt_ref[...] = gbuf[...]
    depth = cbuf.shape[1]
    for d in range(wide * grp):
        src_ref[d * depth : d * depth + depth, :] = cbuf[d]
    group = grp * slots
    width = list_ref.shape[1]
    first = jnp.concatenate([cbuf[d, 0:1, :] for d in range(wide * grp)], axis=0)
    source_row = lax.broadcasted_iota(jnp.int32, (wide * grp, width), 0)
    source_col = lax.broadcasted_iota(jnp.int32, (wide * grp, width), 1)
    living = jnp.zeros((1, width), jnp.float32)
    for c in range(slots):
        flag = first[:, packs * stride + c : packs * stride + c + 1]
        living = living + jnp.sum(
            jnp.where(source_col == source_row * slots + c, flag, 0.0), axis=0, keepdims=True
        )
    wanted = jnp.concatenate(
        [gbuf[g, 3 * slots : 4 * slots, 0:width] for g in range(grp)], axis=0
    )
    slot_row = lax.broadcasted_iota(jnp.int32, (group, width), 0) + me_w * group
    slot_col = lax.broadcasted_iota(jnp.int32, (group, width), 1)
    wanted = jnp.where((wanted * living > 0.0) & (slot_row != slot_col), 1.0, 0.0)
    before = lax.broadcasted_iota(jnp.int32, (width, width), 0)
    after = lax.broadcasted_iota(jnp.int32, (width, width), 1)
    lower = jnp.where(before < after, 1.0, 0.0).astype(jnp.bfloat16)
    rank = jnp.dot(wanted.astype(jnp.bfloat16), lower, preferred_element_type=jnp.float32)
    rank = jnp.where(wanted > 0.0, rank, -1.0)
    rank_cols = jnp.transpose(rank)
    seat = lax.broadcasted_iota(jnp.int32, (caps, width), 1).astype(jnp.float32)
    name = (lax.broadcasted_iota(jnp.int32, (caps, width), 0) - caps).astype(jnp.float32)
    for t in range(group):
        here = jnp.where(rank_cols[0:caps, t : t + 1] == seat, name, 0.0)
        ids = jnp.sum(here, axis=0, keepdims=True) + caps
        list_ref[t : t + 1, :] = ids.astype(jnp.int32)
    counts = jnp.sum(wanted, axis=1, keepdims=True)
    list_ref[group : 2 * group, :] = jnp.broadcast_to(counts, (group, width)).astype(jnp.int32)
    list_ref[2 * group : 2 * group + 8, :] = jnp.broadcast_to(living, (8, width)).astype(jnp.int32)


def pair_kernel(
    slots, grp, wide, rows, stride, packs,
    list_ref, ops_ref, tgt_ref, src_ref,
    out_ref, acc_ref, ops_buf, ops_sem, spread, flip, aim, heap, sems,
):
    lanes = tgt_ref.shape[2]
    group = grp * slots
    caps = wide * group
    loads = [
        pltpu.make_async_copy(ops_ref.at[c], ops_buf.at[c], ops_sem.at[c]) for c in range(slots)
    ]
    for load in loads:
        load.start()
    copies = []
    for c in range(slots):
        for a in range(3):
            for b in range(3):
                index = SYM.index((min(a, b), max(a, b)))
                copies.append(
                    pltpu.make_async_copy(
                        ops_buf.at[c, index], out_ref.at[c, a, b], sems.at[len(copies)]
                    )
                )
    for t in range(group):
        for a in range(3):
            row = a * slots + t % slots
            aim[t, a] = jnp.broadcast_to(tgt_ref[t // slots, row : row + 1, :], (8, lanes))
    spread[caps] = jnp.zeros_like(spread[caps])
    depth = src_ref.shape[0] // (wide * grp)
    batch = 128 // up(depth, 4)
    for lead in range(0, wide * grp, batch):
        many = min(batch, wide * grp - lead)
        flip[:, 0 : many * depth] = jnp.transpose(src_ref[lead * depth : (lead + many) * depth, :])
        for near in range(many):
            for c in range(slots):
                slot = (lead + near) * slots + c

                @pl.when(list_ref[2 * group, slot] > 0)
                def _():
                    for k in range(6):
                        r, q = divmod(c * 6 + k, packs)
                        column = near * depth + r
                        spread[slot, k] = jnp.broadcast_to(
                            flip[q * stride : q * stride + stride, column : column + 1],
                            (stride, 128),
                        )

    for load in loads:
        load.wait()
    for copy in copies:
        copy.start()
    tiles = lanes // 128

    def one_target(t, carry):
        xs = [
            [aim[t, a, :, l * 128 : l * 128 + 128] for a in range(3)] for l in range(tiles)
        ]

        def step(p, sums):
            sums = list(sums)
            for half in range(2):
                s = list_ref[t, 2 * p + half]
                for j in range(0, stride, 8):
                    y = [spread[s, a, j : j + 8, :] for a in range(3)]
                    f = [spread[s, 3 + a, j : j + 8, :] for a in range(3)]
                    for l in range(tiles):
                        d = [xs[l][a] - y[a] for a in range(3)]
                        dist = (d[0] * d[0] + d[1] * d[1]) + d[2] * d[2] + soft_square
                        inv = lax.rsqrt(dist)
                        cube = inv * inv * inv
                        dot = d[0] * f[0] + d[1] * f[1] + d[2] * f[2]
                        near = (dist + soft_square) * cube
                        far = dot * cube
                        for a in range(3):
                            sums[l * 3 + a] = sums[l * 3 + a] + (f[a] * near + d[a] * far)
            return tuple(sums)

        zero = tuple(jnp.zeros((8, 128), jnp.float32) for _ in range(3 * tiles))
        sums = lax.fori_loop(0, (list_ref[group + t, 0] + 1) // 2, step, zero)
        for l in range(tiles):
            for a in range(3):
                heap[t, a, :, l * 128 : l * 128 + 128] = sums[l * 3 + a]
        return carry

    lax.fori_loop(0, group, one_target, 0)
    for t in range(group):
        for a in range(3):
            row = (a * slots + t % slots) * tiles
            whole = jnp.sum(heap[t, a], axis=0, keepdims=True)
            for l in range(tiles):
                acc_ref[t // slots, row + l : row + l + 1, :] = whole[:, l * 128 : l * 128 + 128]
    for copy in copies:
        copy.wait()


def scatter_kernel(slots, grp, part_ref, self_ref, live_ref, vel_ref, got, send, recv):
    n = self_ref.shape[2]
    tiles = part_ref.shape[1] // (3 * slots)
    me = lax.axis_index("grp")
    barrier = pltpu.get_barrier_semaphore()
    for off in range(1, grp):
        pl.semaphore_signal(
            barrier, inc=1, device_id={"grp": lax.rem(me + off, grp)}, device_id_type=MESH
        )
    pl.semaphore_wait(barrier, grp - 1)
    copies = []
    for off in range(1, grp):
        peer = lax.rem(me + off, grp)
        copies.append(
            pltpu.make_async_remote_copy(
                src_ref=part_ref.at[peer],
                dst_ref=got.at[off],
                send_sem=send.at[off],
                recv_sem=recv.at[off],
                device_id={"grp": peer},
                device_id_type=MESH,
            )
        )
    for copy in copies:
        copy.start()
    total = part_ref[me]
    for index, copy in enumerate(copies):
        copy.wait()
        total = total + got[index + 1]
    for a in range(3):
        for c in range(slots):
            row = (a * slots + c) * tiles
            line = jnp.concatenate([total[row + l : row + l + 1] for l in range(tiles)], axis=1)
            value = self_ref[a, c : c + 1, :] + line[:, :n]
            vel_ref[a, c : c + 1, :] = value * live_ref[c].astype(jnp.float32)


def on_device(shapes, density, quad_weight, live, neighbor, rotation):
    slots, _, n = shapes.shape
    caps = neighbor.shape[1]
    grp = lax.axis_size("grp")
    wide = lax.axis_size("wide")
    group = grp * slots
    rows = up(4 * slots, 8)
    lanes = up(max(n, caps), 128)
    width = up(caps, 128)
    tall = up(n, 16)
    chunk = -(-n // grp)
    stride = up(chunk, 8)
    span = 128
    packs = (span - slots) // stride
    depth = -(-6 * slots // packs)
    flat_shapes = shapes.transpose(1, 0, 2)
    flat_density = density.transpose(1, 0, 2)
    vmem = pl.BlockSpec(memory_space=pltpu.VMEM)
    smem = pl.BlockSpec(memory_space=pltpu.SMEM)
    any_space = pl.BlockSpec(memory_space=pl.ANY)
    ops6, self_velocity, targets, sources, lists = pl.pallas_call(
        functools.partial(gather_kernel, slots, grp, wide, rows, chunk, stride, packs),
        out_shape=(
            jax.ShapeDtypeStruct((slots, 6, n, n), jnp.bfloat16),
            jax.ShapeDtypeStruct((3, slots, n), jnp.float32),
            jax.ShapeDtypeStruct((grp, rows, lanes), jnp.float32),
            jax.ShapeDtypeStruct((wide * grp * depth, span), jnp.float32),
            jax.ShapeDtypeStruct((2 * group + 8, width), jnp.int32),
        ),
        in_specs=[vmem, vmem, vmem, smem, vmem, vmem],
        out_specs=(any_space,) + (vmem,) * 4,
        scratch_shapes=[
            pltpu.VMEM((slots, 6, n, n), jnp.bfloat16),
            pltpu.SemaphoreType.DMA((slots,)),
            pltpu.VMEM((rows, lanes), jnp.float32),
            pltpu.VMEM((slots, 8, lanes), jnp.float32),
            pltpu.VMEM((grp, depth, span), jnp.float32),
            pltpu.VMEM((grp, rows, lanes), jnp.float32),
            pltpu.VMEM((wide * grp, depth, span), jnp.float32),
            pltpu.VMEM((6, tall, n), jnp.bfloat16),
            pltpu.VMEM((lanes, 8), jnp.float32),
            pltpu.VMEM((n, lanes + 8), jnp.bfloat16),
            pltpu.VMEM((lanes, 8), jnp.float32),
            pltpu.SemaphoreType.DMA((grp,)),
            pltpu.SemaphoreType.DMA((grp,)),
            pltpu.SemaphoreType.DMA((wide * grp,)),
            pltpu.SemaphoreType.DMA((wide * grp,)),
        ],
        compiler_params=pltpu.CompilerParams(collective_id=0, has_side_effects=True),
        name="gather_ops",
    )(flat_shapes, flat_density, quad_weight, live, neighbor, rotation)
    blocks, partial = pl.pallas_call(
        functools.partial(pair_kernel, slots, grp, wide, rows, stride, packs),
        out_shape=(
            jax.ShapeDtypeStruct((slots, 3, 3, n, n), jnp.bfloat16),
            jax.ShapeDtypeStruct((grp, 3 * slots * lanes // 128, 128), jnp.float32),
        ),
        in_specs=[smem, any_space, vmem, vmem],
        out_specs=(any_space, vmem),
        scratch_shapes=[
            pltpu.VMEM((slots, 6, n, n), jnp.bfloat16),
            pltpu.SemaphoreType.DMA((slots,)),
            pltpu.VMEM((caps + 1, 6, stride, 128), jnp.float32),
            pltpu.VMEM((span, 128), jnp.float32),
            pltpu.VMEM((group, 3, 8, lanes), jnp.float32),
            pltpu.VMEM((group, 3, 8, lanes), jnp.float32),
            pltpu.SemaphoreType.DMA((9 * slots,)),
        ],
        name="pair_sums",
    )(lists, ops6, targets, sources)
    velocity = pl.pallas_call(
        functools.partial(scatter_kernel, slots, grp),
        out_shape=jax.ShapeDtypeStruct((3, slots, n), jnp.float32),
        in_specs=[vmem, vmem, smem],
        out_specs=vmem,
        scratch_shapes=[
            pltpu.VMEM((grp, 3 * slots * lanes // 128, 128), jnp.float32),
            pltpu.SemaphoreType.DMA((grp,)),
            pltpu.SemaphoreType.DMA((grp,)),
        ],
        compiler_params=pltpu.CompilerParams(collective_id=1, has_side_effects=True),
        name="scatter_sums",
    )(partial, self_velocity, live)
    return (blocks.transpose(0, 1, 3, 2, 4), velocity.transpose(1, 0, 2))


def solution(mesh):
    placed = (
        P(("wide", "grp"), None, None),
        P(("wide", "grp"), None, None),
        P(("wide", "grp"), None),
        P(("wide", "grp")),
        P(("wide", "grp"), None),
        P(),
    )
    return jax.shard_map(
        on_device,
        mesh=mesh,
        in_specs=placed,
        out_specs=(P(("wide", "grp"), None, None, None, None), P(("wide", "grp"), None, None)),
        check_vma=False,
    )
```

profile of v0, /device:TPU:0, one launch (start us, length us, event | category | flops | bytes accessed | tf_op | source)
XLA Modules:
  0.0 39.1 jit_solution(10236982586662536017)
XLA Ops:
  0.6 16.5 %gather_ops.1 = (bf16[2,6,312,312]{3,2,1,0:T(8,128)(2,1)}, f32[3,2,312]{2,1,0:T(2,128)}, f32[8,8,384]{2,1,0:T(8,128)}, f32[128,128]{1,0:T(8,128)}, s32[40,128]{1,0:T(8,128)}) custom-call(f32[3,2,312]{2,1,0:T(2,128)} %bitcast.5, f32[3,2,312]{2,1,0:T(2,128)} %bitcast.6, f32[2,312]{1,0:T(2,128)} %qw_ref.1, s32[2]{0:T(128)} %live_ref.3, s32[2,64]{1,0:T(2,128)} %nbr_ref.1, ...), custom_call_target="tpu_custom_call" | custom-call | tf_op jit(solution)/shard_map/gather_ops/pallas_call | solution.py:354
  17.1 13.4 %pair_sums.1 = (bf16[2,3,3,312,312]{4,3,2,1,0:T(8,128)(2,1)}, f32[8,18,128]{2,1,0:T(8,128)}) custom-call(s32[40,128]{1,0:T(8,128)} %get-tuple-element.9.list_ref, bf16[2,6,312,312]{3,2,1,0:T(8,128)(2,1)} %get-tuple-element.10.ops_ref, f32[8,8,384]{2,1,0:T(8,128)} %get-tuple-element.11.tgt_ref, f32[128,128]{1,0:T(8,128)} %get-tuple-element.12.src_ref), custom_call_target="tpu_custom_call" | custom-call | tf_op jit(solution)/shard_map/pair_sums/pallas_call | solution.py:385
  30.5 7.2 %scatter_sums.1 = f32[3,2,312]{2,1,0:T(2,128)} custom-call(f32[8,18,128]{2,1,0:T(8,128)} %get-tuple-element.14.part_ref, f32[3,2,312]{2,1,0:T(2,128)} %get-tuple-element.15.self_ref, s32[2]{0:T(128)} %live_ref.3), custom_call_target="tpu_custom_call" | custom-call | tf_op jit(solution)/shard_map/scatter_sums/pallas_call | solution.py:404
  37.8 1.3 %copy.9 = f32[2,3,312]{2,0,1:T(2,128)} copy(f32[2,3,312]{2,0,1:T(2,128)} %bitcast.4) | data formatting | bytes 14976
where the time goes:
time: 39.1 us
  Pallas kernels  37.1 us (95%)
  local copies, waits for them, and re-layouts  1.3 us (3%)
  between operations  0.65 us (2%)
    pallas_call x1, Pallas kernels, on_device(): pl.pallas_call(functools.partial(gather_kernel, slots, grp, wide, rows, c...  16.5 us
    pallas_call x1, Pallas kernels, on_device(): pl.pallas_call(functools.partial(pair_kernel, slots, grp, wide, rows, str...  13.4 us
    pallas_call x1, Pallas kernels, on_device(): pl.pallas_call(functools.partial(scatter_kernel, slots, grp), out_shape=j...  7.25 us
    unnamed x1, local copies, waits for them, and re-layouts  1.3 us

commit v1 on v0

--- a/solution.py
+++ b/solution.py
@@ -202,7 +202,7 @@
 def pair_kernel(
     slots, grp, wide, rows, stride, packs,
     list_ref, ops_ref, tgt_ref, src_ref,
-    out_ref, acc_ref, ops_buf, ops_sem, spread, flip, aim, heap, sems,
+    out_ref, acc_ref, acc, ops_buf, ops_sem, spread, flip, aim, heap, sems,
 ):
     lanes = tgt_ref.shape[2]
     group = grp * slots
@@ -289,7 +289,8 @@
             row = (a * slots + t % slots) * tiles
             whole = jnp.sum(heap[t, a], axis=0, keepdims=True)
             for l in range(tiles):
-                acc_ref[t // slots, row + l : row + l + 1, :] = whole[:, l * 128 : l * 128 + 128]
+                acc[t // slots, row + l : row + l + 1, :] = whole[:, l * 128 : l * 128 + 128]
+    acc_ref[...] = acc[...].astype(acc_ref.dtype)
     for copy in copies:
         copy.wait()
 
@@ -319,10 +320,10 @@
         )
     for copy in copies:
         copy.start()
-    total = part_ref[me]
+    total = part_ref[me].astype(jnp.float32)
     for index, copy in enumerate(copies):
         copy.wait()
-        total = total + got[index + 1]
+        total = total + got[index + 1].astype(jnp.float32)
     for a in range(3):
         for c in range(slots):
             row = (a * slots + c) * tiles
@@ -386,11 +387,12 @@
         functools.partial(pair_kernel, slots, grp, wide, rows, stride, packs),
         out_shape=(
             jax.ShapeDtypeStruct((slots, 3, 3, n, n), jnp.bfloat16),
-            jax.ShapeDtypeStruct((grp, 3 * slots * lanes // 128, 128), jnp.float32),
+            jax.ShapeDtypeStruct((grp, 3 * slots * lanes // 128, 128), jnp.bfloat16),
         ),
         in_specs=[smem, any_space, vmem, vmem],
         out_specs=(any_space, vmem),
         scratch_shapes=[
+            pltpu.VMEM((grp, 3 * slots * lanes // 128, 128), jnp.float32),
             pltpu.VMEM((slots, 6, n, n), jnp.bfloat16),
             pltpu.SemaphoreType.DMA((slots,)),
             pltpu.VMEM((caps + 1, 6, stride, 128), jnp.float32),
@@ -407,7 +409,7 @@
         in_specs=[vmem, vmem, smem],
         out_specs=vmem,
         scratch_shapes=[
-            pltpu.VMEM((grp, 3 * slots * lanes // 128, 128), jnp.float32),
+            pltpu.VMEM((grp, 3 * slots * lanes // 128, 128), jnp.bfloat16),
             pltpu.SemaphoreType.DMA((grp,)),
             pltpu.SemaphoreType.DMA((grp,)),
         ],

time: 39.1 us -> 38.4 us (0.982)
  Pallas kernels: 37.1 us -> 36.4 us
    pallas_call x1, Pallas kernels: 13.4 us -> 12.8 us  [on_device(): pl.pallas_call(functools.partial(pair_kernel, slots, grp, wide, rows, str...]
where the time goes in v1:
time: 38.4 us
  Pallas kernels  36.4 us (95%)
  local copies, waits for them, and re-layouts  1.3 us (3%)
  between operations  0.65 us (2%)
    pallas_call x1, Pallas kernels, on_device(): pl.pallas_call(functools.partial(gather_kernel, slots, grp, wide, rows, c...  16.5 us
    pallas_call x1, Pallas kernels, on_device(): pl.pallas_call(functools.partial(pair_kernel, slots, grp, wide, rows, str...  12.8 us
    pallas_call x1, Pallas kernels, on_device(): pl.pallas_call(functools.partial(scatter_kernel, slots, grp), out_shape=j...  7.1 us
    unnamed x1, local copies, waits for them, and re-layouts  1.3 us

profile of v1, /device:TPU:0, one launch (start us, length us, event | category | flops | bytes accessed | tf_op | source)
XLA Modules:
  0.0 38.4 jit_solution(14335772430798615098)
XLA Ops:
  0.6 16.5 %gather_ops.1 = (bf16[2,6,312,312]{3,2,1,0:T(8,128)(2,1)}, f32[3,2,312]{2,1,0:T(2,128)}, f32[8,8,384]{2,1,0:T(8,128)}, f32[128,128]{1,0:T(8,128)}, s32[40,128]{1,0:T(8,128)}) custom-call(f32[3,2,312]{2,1,0:T(2,128)} %bitcast.5, f32[3,2,312]{2,1,0:T(2,128)} %bitcast.6, f32[2,312]{1,0:T(2,128)} %qw_ref.1, s32[2]{0:T(128)} %live_ref.3, s32[2,64]{1,0:T(2,128)} %nbr_ref.1, ...), custom_call_target="tpu_custom_call" | custom-call | tf_op jit(solution)/shard_map/gather_ops/pallas_call | solution.py:355
  17.1 12.8 %pair_sums.1 = (bf16[2,3,3,312,312]{4,3,2,1,0:T(8,128)(2,1)}, bf16[8,18,128]{2,1,0:T(8,128)(2,1)}) custom-call(s32[40,128]{1,0:T(8,128)} %get-tuple-element.9.list_ref, bf16[2,6,312,312]{3,2,1,0:T(8,128)(2,1)} %get-tuple-element.10.ops_ref, f32[8,8,384]{2,1,0:T(8,128)} %get-tuple-element.11.tgt_ref, f32[128,128]{1,0:T(8,128)} %get-tuple-element.12.src_ref), custom_call_target="tpu_custom_call" | custom-call | tf_op jit(solution)/shard_map/pair_sums/pallas_call | solution.py:386
  30.0 7.1 %scatter_sums.1 = f32[3,2,312]{2,1,0:T(2,128)} custom-call(bf16[8,18,128]{2,1,0:T(8,128)(2,1)} %get-tuple-element.14.part_ref, f32[3,2,312]{2,1,0:T(2,128)} %get-tuple-element.15.self_ref, s32[2]{0:T(128)} %live_ref.3), custom_call_target="tpu_custom_call" | custom-call | tf_op jit(solution)/shard_map/scatter_sums/pallas_call | solution.py:406
  37.1 1.3 %copy.9 = f32[2,3,312]{2,0,1:T(2,128)} copy(f32[2,3,312]{2,0,1:T(2,128)} %bitcast.4) | data formatting | bytes 14976
